TPU v7x, 32 devices: a whole 2x2x4 slice. The times are simulated.
32 devices in a mesh: seq: 4 (over y, x), span: 4 (over z), kvg: 2 (over core).
Axes of the slice: x: 2, y: 2, z: 4, core: 2. Of those that a mesh axis runs over, the one named last changes fastest.
Arguments:
- query_rows: bfloat16 [8704, 1792], P(('seq', 'span'), 'kvg'), parts along dimension 0, may hold values from -256 to 256
- key_rows: bfloat16 [8704, 256], P(('seq', 'span'), 'kvg'), parts along dimension 0, may hold values from -6 to 6
- value_rows: bfloat16 [8704, 256], P(('seq', 'span'), 'kvg'), parts along dimension 0, may hold values from -6 to 6
- out_grad: bfloat16 [8704, 1792], P(('seq', 'span'), 'kvg'), parts along dimension 0, may hold values from -6 to 6
- ratios: int32 [16], P('seq'), parts along dimension 0, may hold values from 16 to 64, as said below
Outputs:
- attended: bfloat16 [8704, 1792], P(('seq', 'span'), 'kvg'), parts along dimension 0
- query_grad: bfloat16 [8704, 1792], P(('seq', 'span'), 'kvg'), parts along dimension 0
- key_grad: bfloat16 [8704, 256], P(('seq', 'span'), 'kvg'), parts along dimension 0
- value_grad: bfloat16 [8704, 256], P(('seq', 'span'), 'kvg'), parts along dimension 0
There are 4 independent parts, one for each index of `seq`. A program takes and returns all parts, laid end to end along the dimension named above; each array names one. Nothing has to cross between parts.
Inputs may be any that keep to these rules, and one draw needn't show every extreme that they name: `ratios`: every ratio is 16, 32 or 64, and some span of every sequence has 16.
All inputs are finite; a program needn't handle non-finite values.
Results may differ from a plain program's by a relative error of at most 0.0096.
Values may be sent and summed in bfloat16 or wider, within the bound.
A program may use at most 64 MiB of HBM per device.

v0:
```python
import jax
import jax.numpy as jnp
from jax import lax
from jax.sharding import PartitionSpec as P

SPAN = 512
HD = 128
QPG = 7
BMAX = 32
SEG = 544
floor_score = -1e30


def product(pattern, first_arg, second_arg):
    return jnp.einsum(pattern, first_arg, second_arg, preferred_element_type=jnp.float32)


def build_masks(ratios, first_span, local_spans):
    counts = SPAN // ratios
    slot_ids = jnp.arange(BMAX, dtype=jnp.int32)
    live_slots = (slot_ids[None, :] < counts[:, None]).reshape(-1)
    span_ids = first_span + jnp.arange(local_spans, dtype=jnp.int32)
    owner_span = jnp.arange(live_slots.shape[0], dtype=jnp.int32) // BMAX
    beacon_mask = (owner_span[None, :] < span_ids[:, None]) & live_slots[None, :]
    local_ratio = lax.dynamic_slice_in_dim(ratios, first_span, local_spans)
    local_count = SPAN // local_ratio
    positions = jnp.arange(SEG, dtype=jnp.int32)
    is_beacon = positions >= SPAN
    slot_of = positions - SPAN
    key_order = jnp.where(
        is_beacon[None, :], (slot_of[None, :] + 1) * local_ratio[:, None] - 1, positions[None, :]
    )
    live_row = jnp.logical_not(is_beacon[None, :]) | (slot_of[None, :] < local_count[:, None])
    raw_key = jnp.logical_not(is_beacon)[None, None, :] & (
        key_order[:, None, :] <= key_order[:, :, None]
    )
    beacon_key = (
        is_beacon[None, :, None]
        & is_beacon[None, None, :]
        & live_row[:, None, :]
        & (positions[None, None, :] <= positions[None, :, None])
    )
    return (beacon_mask, raw_key | beacon_key, live_row.astype(jnp.float32))


def attend_head(
    query_head,
    grad_head,
    beacon_keys,
    beacon_values,
    own_keys,
    own_values,
    beacon_mask,
    own_mask,
    live_rows,
):
    score_scale = HD ** (-0.5)
    beacon_scores = jnp.where(
        beacon_mask[:, None, :],
        product("csd,bd->csb", query_head, beacon_keys) * score_scale,
        floor_score,
    )
    own_scores = jnp.where(
        own_mask, product("csd,ctd->cst", query_head, own_keys) * score_scale, floor_score
    )
    row_top = jnp.maximum(jnp.max(beacon_scores, -1), jnp.max(own_scores, -1))
    row_total = jnp.sum(jnp.exp(beacon_scores - row_top[..., None]), -1) + jnp.sum(
        jnp.exp(own_scores - row_top[..., None]), -1
    )
    row_lse = row_top + jnp.log(row_total)
    beacon_probs = jnp.exp(beacon_scores - row_lse[..., None])
    own_probs = jnp.exp(own_scores - row_lse[..., None])
    beacon_weights = beacon_probs.astype(jnp.bfloat16)
    own_weights = own_probs.astype(jnp.bfloat16)
    mixed_rows = product("csb,bd->csd", beacon_weights, beacon_values) + product(
        "cst,ctd->csd", own_weights, own_values
    )
    attended = (mixed_rows * live_rows[..., None]).astype(jnp.bfloat16)
    grad_rows = grad_head * live_rows.astype(jnp.bfloat16)[..., None]
    row_delta = jnp.sum(grad_rows.astype(jnp.float32) * attended.astype(jnp.float32), -1)
    beacon_sgrad = (
        beacon_probs * (product("csd,bd->csb", grad_rows, beacon_values) - row_delta[..., None])
    ).astype(jnp.bfloat16)
    own_sgrad = (
        own_probs * (product("csd,ctd->cst", grad_rows, own_values) - row_delta[..., None])
    ).astype(jnp.bfloat16)
    query_grad = (
        score_scale
        * (
            product("csb,bd->csd", beacon_sgrad, beacon_keys)
            + product("cst,ctd->csd", own_sgrad, own_keys)
        )
    ).astype(jnp.bfloat16)
    beacon_kgrad = score_scale * product("csb,csd->bd", beacon_sgrad, query_head)
    beacon_vgrad = product("csb,csd->bd", beacon_weights, grad_rows)
    own_kgrad = score_scale * product("cst,csd->ctd", own_sgrad, query_head)
    own_vgrad = product("cst,csd->ctd", own_weights, grad_rows)
    return (attended, query_grad, beacon_kgrad, beacon_vgrad, own_kgrad, own_vgrad)


def local(query_rows, key_rows, value_rows, out_grad, ratios):
    span_index = lax.axis_index("span")
    local_spans = query_rows.shape[0] // SEG
    groups = key_rows.shape[1] // HD
    beacon_count = ratios.shape[0] * BMAX
    first_span = span_index * local_spans
    beacon_mask, own_mask, live_rows = build_masks(ratios, first_span, local_spans)
    query_blocks = query_rows.reshape(local_spans, SEG, groups, QPG, HD)
    grad_blocks = out_grad.reshape(local_spans, SEG, groups, QPG, HD)
    key_blocks = key_rows.reshape(local_spans, SEG, groups, HD)
    value_blocks = value_rows.reshape(local_spans, SEG, groups, HD)
    own_pair = jnp.concatenate(
        [
            key_blocks[:, SPAN:].reshape(local_spans * BMAX, groups * HD),
            value_blocks[:, SPAN:].reshape(local_spans * BMAX, groups * HD),
        ],
        1,
    )
    beacon_pairs = lax.all_gather(own_pair, "span", axis=0, tiled=True)
    attended_parts, query_parts, term_keys, term_values, own_key_parts, own_value_parts = (
        [],
        [],
        [],
        [],
        [],
        [],
    )
    own_keys = key_blocks[:, :, 0]
    own_values = value_blocks[:, :, 0]
    beacon_keys = beacon_pairs[:, 0:HD]
    beacon_values = beacon_pairs[:, groups * HD : (groups + 1) * HD]
    beacon_ksum = jnp.zeros((beacon_count, HD), jnp.float32)
    beacon_vsum = jnp.zeros((beacon_count, HD), jnp.float32)
    own_ksum = jnp.zeros((local_spans, SEG, HD), jnp.float32)
    own_vsum = jnp.zeros((local_spans, SEG, HD), jnp.float32)
    head_outputs = []
    head_grads = []
    for head_index in range(QPG):
        result = attend_head(
            query_blocks[:, :, 0, head_index],
            grad_blocks[:, :, 0, head_index],
            beacon_keys,
            beacon_values,
            own_keys,
            own_values,
            beacon_mask,
            own_mask,
            live_rows,
        )
        head_outputs.append(result[0])
        head_grads.append(result[1])
        beacon_ksum = beacon_ksum + result[2]
        beacon_vsum = beacon_vsum + result[3]
        own_ksum = own_ksum + result[4]
        own_vsum = own_vsum + result[5]
    attended_parts.append(jnp.stack(head_outputs, 2))
    query_parts.append(jnp.stack(head_grads, 2))
    term_keys.append(beacon_ksum)
    term_values.append(beacon_vsum)
    own_key_parts.append(own_ksum)
    own_value_parts.append(own_vsum)
    grad_term = jnp.concatenate(term_keys + term_values, 1)
    own_sums = lax.psum_scatter(grad_term, "span", scatter_dimension=0, tiled=True)
    own_sums = own_sums.reshape(local_spans, BMAX, 2 * groups, HD)
    own_key = jnp.stack(own_key_parts, 2)
    own_value = jnp.stack(own_value_parts, 2)
    key_total = jnp.concatenate([own_key[:, :SPAN], own_key[:, SPAN:] + own_sums[:, :, :groups]], 1)
    value_total = jnp.concatenate(
        [own_value[:, :SPAN], own_value[:, SPAN:] + own_sums[:, :, groups:]], 1
    )
    attended = jnp.stack(attended_parts, 2).reshape(local_spans * SEG, groups * QPG * HD)
    query_grad = jnp.stack(query_parts, 2).reshape(local_spans * SEG, groups * QPG * HD)
    key_grad = key_total.astype(jnp.bfloat16).reshape(local_spans * SEG, groups * HD)
    value_grad = value_total.astype(jnp.bfloat16).reshape(local_spans * SEG, groups * HD)
    return (attended, query_grad, key_grad, value_grad)


def solution(mesh):
    placed = (
        P(("seq", "span"), "kvg"),
        P(("seq", "span"), "kvg"),
        P(("seq", "span"), "kvg"),
        P(("seq", "span"), "kvg"),
        P("seq"),
    )
    return jax.shard_map(
        local,
        mesh=mesh,
        in_specs=placed,
        out_specs=(
            P(("seq", "span"), "kvg"),
            P(("seq", "span"), "kvg"),
            P(("seq", "span"), "kvg"),
            P(("seq", "span"), "kvg"),
        ),
        check_vma=False,
    )
```

profile of v0, /device:TPU:0, one launch (start us, length us, event | category | flops | bytes accessed | tf_op | source)
XLA Modules:
  0.0 112.2 jit_solution(4719098975755676397)
XLA Ops:
  7.2 1.2 %dynamic_slice.3 = s32[1]{0:T(128)} dynamic-slice(s32[4]{0:T(128)} %param.9, s32[]{:T(128)S(6)} %select_n.105), dynamic_slice_sizes={1} | dynamic-slice | bytes 12 | tf_op jit(solution)/shard_map/dynamic_slice | solution.py:25
  10.4 0.8 and_select_fusion
  11.9 2.2 %reshape.1308 = bf16[1,544,1,7,128]{4,3,1,2,0:T(8,128)(2,1)S(1)} reshape(bf16[544,896]{1,0:T(8,128)(2,1)} %param.5) | data formatting | bytes 1949696 | tf_op jit(solution)/shard_map/reshape | solution.py:108
  14.2 2.4 %fusion.265 = (bf16[1,544,1,1,128]{4,3,1,2,0:T(2,128)(2,1)S(1)}, bf16[1,544,1,1,128]{4,3,1,2,0:T(2,128)(2,1)S(1)}, bf16[1,544,1,1,128]{4,3,1,2,0:T(2,128)(2,1)},...) fusion(bf16[1,544,1,7,128]{4,3,1,2,0:T(8,128)(2,1)S(1)} %reshap, ...), kind=kLoop, calls=%fused_computation.404 | loop fusion | bytes 1949696 | tf_op jit(solution)/shard_map/slice | solution.py:140
  16.6 15.1 %all_gather.3 = bf16[128,256]{1,0:T(8,128)(2,1)S(1)} all-gather(bf16[32,256]{1,0:T(8,128)(2,1)S(1)} %pad_maximum_fusion.3), channel_id=1, replica_groups=mesh['seq'=4,'span'=4,'kvg'=2] {'span'}, dimensions={0}, use_global_device_ids=true | all-gather | bytes 81920 | tf_op jit(solution)/shard_map/all_gather | solution.py:119
  32.6 1.4 %fusion.278 = (f32[544]{0:T(1024)S(1)}, f32[544,544]{0,1:T(8,128)S(1)}) fusion(bf16[544,128]{1,0:T(8,128)(2,1)S(1)} %copy-done.16, bf16[1,544,1,1,128]{4,1,3,2,0:T(8,128)(2,1)S(1)} %copy.71, pred[544]{0:T(1024)(128)(4,1)} %copy-done.124, pred[544]{0:T(1024)(128)(4,1)S(1)} %get-tuple-element.80, s32[544]{0:T(1024)S(1)} %iota_select_fusion, ...), kind=kOutput, calls=%fused_computation.417 | convolution fusion | flops 78718432 | bytes 1468256 | tf_op jit(solution)/shard_map/csd,ctd->cst/dot_general | solution.py:15
  34.8 1.4 %fusion.276 = (f32[544]{0:T(1024)S(1)}, f32[544,544]{0,1:T(8,128)S(1)}) fusion(bf16[544,128]{1,0:T(8,128)(2,1)S(1)} %copy-done.16, bf16[1,544,1,1,128]{4,1,3,2,0:T(8,128)(2,1)S(1)} %copy.70, pred[544]{0:T(1024)(128)(4,1)S(1)} %copy-done.125, pred[544]{0:T(1024)(128)(4,1)} %copy-done.122, s32[544]{0:T(1024)S(1)} %iota_select_fusion, ...), kind=kOutput, calls=%fused_computation.415 | convolution fusion | flops 78718432 | bytes 1468256 | tf_op jit(solution)/shard_map/csd,ctd->cst/dot_general | solution.py:15
  42.4 1.0 fusion.229
  43.9 1.0 fusion.231
  45.4 1.0 fusion.233
  47.0 1.0 fusion.235
  48.5 1.0 fusion.237
  50.0 1.0 fusion.239
  52.1 1.0 fusion.241
  53.0 3.0 %reshape.1316 = bf16[1,544,1,7,128]{4,3,1,2,0:T(8,128)(2,1)} reshape(bf16[544,896]{1,0:T(8,128)(2,1)} %param.8) | data formatting | bytes 1949696 | tf_op jit(solution)/shard_map/reshape | solution.py:109
  56.1 6.1 %fusion.264 = (bf16[1,544,1,1,128]{4,3,1,2,0:T(2,128)(2,1)S(1)}, bf16[1,544,1,1,128]{4,3,1,2,0:T(2,128)(2,1)S(1)}, bf16[1,544,1,1,128]{4,3,1,2,0:T(2,128)(2,1)S(...) fusion(bf16[1,544,1,7,128]{4,3,1,2,0:T(8,128)(2,1)} %reshape.1316), kind=kLoop, calls=%fused_computation.403 | loop fusion | bytes 1949696 | tf_op jit(solution)/shard_map/slice | solution.py:141
  62.7 0.8 copy-done.11
  64.7 0.7 copy-done.5
  68.1 0.9 copy-done.61
  69.1 0.9 multiply_reduce_fusion
  78.1 0.8 copy.64
  78.9 1.9 %fusion.109 = f32[544,128]{1,0:T(8,128)S(1)} fusion(f32[544,544]{0,1:T(8,128)} %copy-done.13, f32[544]{0:T(1024)S(1)} %copy-done.109, bf16[1,544,1,1,128]{4,1,3,2,0:T(8,128)(2,1)S(1)} %copy-done.60, bf16[544]{0:T(1024)(128)(2,1)S(1)} %get-tuple-element.76), kind=kOutput, calls=%fused_computation.210 | convolution fusion | flops 76421120 | bytes 1604800 | tf_op jit(solution)/shard_map/cst,csd->ctd/dot_general | solution.py:15
  81.4 0.8 copy-done.12
  82.7 0.8 copy-done.9
  84.1 0.8 copy-done.6
  85.4 0.9 copy-done.3
  87.2 0.7 fusion.17
  99.9 1.1 copy.93
  101.8 1.1 copy.94
  102.9 0.9 copy.65
  104.0 0.7 pad_maximum_fusion.1
  104.6 0.7 pad_maximum_fusion
  (379 shorter events, 39.0 us)
Async XLA Ops:
  7.2 95.8 %reduce-scatter.4.cloned.1.call-start = ((), (), s32[]{:S(2)}) async-start(), calls=%async_computation.1 | async-start | bytes 163840
  10.4 21.5 %copy-start.126 = (pred[544]{0:T(1024)(128)(4,1)}, pred[544]{0:T(1024)(128)(4,1)S(1)}, u32[]{:S(2)}) copy-start(pred[544]{0:T(1024)(128)(4,1)S(1)} %fusion.220) | copy-start | bytes 1636
  11.3 20.7 %copy-start.124 = (pred[544]{0:T(1024)(128)(4,1)}, pred[544]{0:T(1024)(128)(4,1)S(1)}, u32[]{:S(2)}) copy-start(pred[544]{0:T(1024)(128)(4,1)S(1)} %get-tuple-element.81) | copy-start | bytes 1636
  11.3 21.3 %copy-start.122 = (pred[544]{0:T(1024)(128)(4,1)}, pred[544]{0:T(1024)(128)(4,1)S(1)}, u32[]{:S(2)}) copy-start(pred[544]{0:T(1024)(128)(4,1)S(1)} %get-tuple-element.80) | copy-start | bytes 1636
  16.6 17.4 %copy-start.29 = (bf16[1,544,1,1,128]{4,1,3,2,0:T(8,128)(2,1)}, bf16[1,544,1,1,128]{4,1,3,2,0:T(8,128)(2,1)S(1)}, u32[]{:S(2)}) copy-start(bf16[1,544,1,1,128]{4,1,3,2,0:T(8,128)(2,1)S(1)} %copy.72) | copy-start | bytes 417796
  34.7 9.2 %copy-start.17 = (f32[128,544]{0,1:T(8,128)}, f32[128,544]{0,1:T(8,128)S(1)}, u32[]{:S(2)}) copy-start(f32[128,544]{0,1:T(8,128)S(1)} %get-tuple-element.65) | copy-start | bytes 835588
  36.2 8.7 %copy-start.1 = (f32[544,544]{0,1:T(8,128)}, f32[544,544]{0,1:T(8,128)S(1)}, u32[]{:S(2)}) copy-start(f32[544,544]{0,1:T(8,128)S(1)} %get-tuple-element.61) | copy-start | bytes 3551236
  36.6 8.9 %copy-start.19 = (f32[128,544]{0,1:T(8,128)}, f32[128,544]{0,1:T(8,128)S(1)}, u32[]{:S(2)}) copy-start(f32[128,544]{0,1:T(8,128)S(1)} %get-tuple-element.59) | copy-start | bytes 835588
  37.5 9.0 %copy-start.4 = (f32[544,544]{0,1:T(8,128)}, f32[544,544]{0,1:T(8,128)S(1)}, u32[]{:S(2)}) copy-start(f32[544,544]{0,1:T(8,128)S(1)} %get-tuple-element.55) | copy-start | bytes 3551236
  37.8 9.1 %copy-start.21 = (f32[128,544]{0,1:T(8,128)}, f32[128,544]{0,1:T(8,128)S(1)}, u32[]{:S(2)}) copy-start(f32[128,544]{0,1:T(8,128)S(1)} %get-tuple-element.53) | copy-start | bytes 835588
  38.7 9.2 %copy-start.7 = (f32[544,544]{0,1:T(8,128)}, f32[544,544]{0,1:T(8,128)S(1)}, u32[]{:S(2)}) copy-start(f32[544,544]{0,1:T(8,128)S(1)} %get-tuple-element.49) | copy-start | bytes 3551236
  39.0 9.4 %copy-start.23 = (f32[128,544]{0,1:T(8,128)}, f32[128,544]{0,1:T(8,128)S(1)}, u32[]{:S(2)}) copy-start(f32[128,544]{0,1:T(8,128)S(1)} %get-tuple-element.47) | copy-start | bytes 835588
  39.9 9.5 %copy-start.10 = (f32[544,544]{0,1:T(8,128)}, f32[544,544]{0,1:T(8,128)S(1)}, u32[]{:S(2)}) copy-start(f32[544,544]{0,1:T(8,128)S(1)} %get-tuple-element.43) | copy-start | bytes 3551236
  40.3 9.7 %copy-start.25 = (f32[128,544]{0,1:T(8,128)}, f32[128,544]{0,1:T(8,128)S(1)}, u32[]{:S(2)}) copy-start(f32[128,544]{0,1:T(8,128)S(1)} %get-tuple-element.41) | copy-start | bytes 835588
  40.9 10.0 %copy-start.13 = (f32[544,544]{0,1:T(8,128)}, f32[544,544]{0,1:T(8,128)S(1)}, u32[]{:S(2)}) copy-start(f32[544,544]{0,1:T(8,128)S(1)} %get-tuple-element.37) | copy-start | bytes 3551236
  41.3 10.2 %copy-start.27 = (f32[128,544]{0,1:T(8,128)}, f32[128,544]{0,1:T(8,128)S(1)}, u32[]{:S(2)}) copy-start(f32[128,544]{0,1:T(8,128)S(1)} %get-tuple-element.35) | copy-start | bytes 835588
  56.1 6.2 %copy-start.14 = (f32[544,544]{0,1:T(8,128)S(1)}, f32[544,544]{0,1:T(8,128)}, u32[]{:S(2)}) copy-start(f32[544,544]{0,1:T(8,128)} %copy-done.13) | copy-start | bytes 3551236
  56.1 6.2 %copy-start.69 = (f32[544,128]{1,0:T(8,128)S(1)}, f32[544,128]{1,0:T(8,128)}, u32[]{:S(2)}) copy-start(f32[544,128]{1,0:T(8,128)} %fusion.241) | copy-start | bytes 835588
  56.1 6.2 %copy-start.108 = (f32[544]{0:T(1024)S(1)}, f32[544]{0:T(1024)}, u32[]{:S(2)}) copy-start(f32[544]{0:T(1024)} %copy-done.107) | copy-start | bytes 6532
  70.0 2.6 %copy-start.57 = (bf16[1,544,1,1,128]{4,1,3,2,0:T(8,128)(2,1)}, bf16[1,544,1,1,128]{4,1,3,2,0:T(8,128)(2,1)S(1)}, u32[]{:S(2)}) copy-start(bf16[1,544,1,1,128]{4,1,3,2,0:T(8,128)(2,1)S(1)} %get-tuple-element.15) | copy-start | bytes 417796
  70.1 3.1 %copy-start.114 = (f32[544]{0:T(1024)}, f32[544]{0:T(1024)S(1)}, u32[]{:S(2)}) copy-start(f32[544]{0:T(1024)S(1)} %get-tuple-element.8) | copy-start | bytes 6532
  70.1 3.4 %copy-start.53 = (bf16[1,544,1,1,128]{4,1,3,2,0:T(8,128)(2,1)}, bf16[1,544,1,1,128]{4,1,3,2,0:T(8,128)(2,1)S(1)}, u32[]{:S(2)}) copy-start(bf16[1,544,1,1,128]{4,1,3,2,0:T(8,128)(2,1)S(1)} %get-tuple-element.13) | copy-start | bytes 417796
  70.1 3.8 %copy-start.112 = (f32[544]{0:T(1024)}, f32[544]{0:T(1024)S(1)}, u32[]{:S(2)}) copy-start(f32[544]{0:T(1024)S(1)} %get-tuple-element.9) | copy-start | bytes 6532
  70.1 4.2 %copy-start.51 = (bf16[1,544,1,1,128]{4,1,3,2,0:T(8,128)(2,1)}, bf16[1,544,1,1,128]{4,1,3,2,0:T(8,128)(2,1)S(1)}, u32[]{:S(2)}) copy-start(bf16[1,544,1,1,128]{4,1,3,2,0:T(8,128)(2,1)S(1)} %get-tuple-element.12) | copy-start | bytes 417796
  70.1 4.6 %copy-start.110 = (f32[544]{0:T(1024)}, f32[544]{0:T(1024)S(1)}, u32[]{:S(2)}) copy-start(f32[544]{0:T(1024)S(1)} %get-tuple-element.10) | copy-start | bytes 6532
  70.1 4.9 %copy-start.49 = (bf16[1,544,1,1,128]{4,1,3,2,0:T(8,128)(2,1)}, bf16[1,544,1,1,128]{4,1,3,2,0:T(8,128)(2,1)S(1)}, u32[]{:S(2)}) copy-start(bf16[1,544,1,1,128]{4,1,3,2,0:T(8,128)(2,1)S(1)} %get-tuple-element.11) | copy-start | bytes 417796
  70.1 5.7 %copy-start.47 = (bf16[1,544,1,1,128]{4,1,3,2,0:T(8,128)(2,1)}, bf16[1,544,1,1,128]{4,1,3,2,0:T(8,128)(2,1)S(1)}, u32[]{:S(2)}) copy-start(bf16[1,544,1,1,128]{4,1,3,2,0:T(8,128)(2,1)S(1)} %get-tuple-element.17) | copy-start | bytes 417796
  71.9 4.4 %copy-start.77 = (bf16[544,128]{1,0:T(8,128)(2,1)}, bf16[544,128]{1,0:T(8,128)(2,1)S(1)}, u32[]{:S(2)}) copy-start(bf16[544,128]{1,0:T(8,128)(2,1)S(1)} %fusion.62) | copy-start | bytes 417796
  72.7 3.9 %copy-start.79 = (bf16[544,128]{1,0:T(8,128)(2,1)}, bf16[544,128]{1,0:T(8,128)(2,1)S(1)}, u32[]{:S(2)}) copy-start(bf16[544,128]{1,0:T(8,128)(2,1)S(1)} %fusion.63) | copy-start | bytes 417796
  73.5 3.4 %copy-start.81 = (bf16[544,128]{1,0:T(8,128)(2,1)}, bf16[544,128]{1,0:T(8,128)(2,1)S(1)}, u32[]{:S(2)}) copy-start(bf16[544,128]{1,0:T(8,128)(2,1)S(1)} %fusion.64) | copy-start | bytes 417796
  74.3 3.0 %copy-start.83 = (bf16[544,128]{1,0:T(8,128)(2,1)}, bf16[544,128]{1,0:T(8,128)(2,1)S(1)}, u32[]{:S(2)}) copy-start(bf16[544,128]{1,0:T(8,128)(2,1)S(1)} %fusion.65) | copy-start | bytes 417796
  77.8 3.0 %copy-start.121 = (f32[544]{0:T(1024)S(1)}, f32[544]{0:T(1024)}, u32[]{:S(2)}) copy-start(f32[544]{0:T(1024)} %copy-done.120) | copy-start | bytes 6532
  (97 other events, 142.2 us)
Sparse Core Ops, SparseCore 0:
  79.0 20.4 reduce-scatter.3
where the time goes:
time: 113 us; the launch traced here: 112 us
  matrix products  40 us (35%)
  local copies, waits for them, and re-layouts  31.5 us (28%)
  between operations  18.1 us (16%)
  blocking collectives  15.1 us (13%)
  other arithmetic  7.4 us (7%)
    dot_general x84, matrix products, product(): jnp.einsum(pattern, first_arg, second_arg, preferred_element_type=jnp.flo...  40 us
    unnamed x269, local copies, waits for them, and re-layouts  15.5 us
    all_gather x1, blocking collectives, local(): beacon_pairs = lax.all_gather(own_pair, 'span', axis=0, tiled=True)  15.1 us
    slice x1, local copies, waits for them, and re-layouts, local(): grad_blocks[:, :, 0, head_index]  6.13 us
    reshape x1, local copies, waits for them, and re-layouts, local(): grad_blocks = out_grad.reshape(local_spans, SEG, groups, QPG, HD)  3.03 us
    slice x1, local copies, waits for them, and re-layouts, local(): query_blocks[:, :, 0, head_index]  2.37 us
  transfers between devices with their start and end apart: 1, of which 0 were waited for; matrix products, arithmetic and copies ran while one was open for 16% of the time, Pallas kernels for 0%

commit v1 on v0

--- a/solution.py
+++ b/solution.py
@@ -116,7 +116,9 @@
         ],
         1,
     )
-    beacon_pairs = lax.all_gather(own_pair, "span", axis=0, tiled=True)
+    beacon_pairs = jnp.concatenate(
+        lax.all_to_all(jnp.stack([own_pair] * lax.axis_size("span")), "span", 0, 0), axis=0
+    )
     attended_parts, query_parts, term_keys, term_values, own_key_parts, own_value_parts = (
         [],
         [],

time: 113 us -> 129 us (1.14)
  matrix products: 40 us -> 59 us
  blocking collectives: 15.1 us -> 0 us
  waiting for transfers between devices: 0.04 us -> 10.3 us
  starting transfers between devices: 0.04 us -> 6.35 us
  local copies, waits for them, and re-layouts: 31.5 us -> 26.7 us
    dot_general x84, matrix products: 40 us -> 59 us  [product(): jnp.einsum(pattern, first_arg, second_arg, preferred_element_type=jnp.flo...]
    all_gather x1 -> x0, blocking collectives: 15.1 us -> none  [local(): beacon_pairs = lax.all_gather(own_pair, 'span', axis=0, tiled=True)]
    unnamed x2, waiting for transfers between devices: 0.04 us -> 10.3 us
    unnamed x269 -> x129, local copies, waits for them, and re-layouts: 15.5 us -> 8.1 us
    all_to_all x0 -> x1, starting transfers between devices: none -> 6.35 us  [local(): lax.all_to_all(jnp.stack([own_pair] * lax.axis_size('span')), 'span', 0, 0)]
  transfers between devices with their start and end apart: 1 -> 2, of which waited for: 0 -> 1; matrix products, arithmetic and copies ran while one was open for 16% -> 33% of each run, Pallas kernels for 0% -> 0%
where the time goes in v1:
time: 129 us; the launch traced here: 128 us
  matrix products  59 us (46%)
  local copies, waits for them, and re-layouts  26.7 us (21%)
  between operations  17.2 us (13%)
  waiting for transfers between devices  10.3 us (8%)
  other arithmetic  8.68 us (7%)
  starting transfers between devices  6.35 us (5%)
    dot_general x84, matrix products, product(): jnp.einsum(pattern, first_arg, second_arg, preferred_element_type=jnp.flo...  59 us
    unnamed x2, waiting for transfers between devices  10.3 us
    unnamed x129, local copies, waits for them, and re-layouts  8.1 us
    slice x1, local copies, waits for them, and re-layouts, local(): grad_blocks[:, :, 0, head_index]  6.81 us
    all_to_all x1, starting transfers between devices, local(): lax.all_to_all(jnp.stack([own_pair] * lax.axis_size('span')), 'span', 0, 0)  6.35 us
    reshape x1, local copies, waits for them, and re-layouts, local(): grad_blocks = out_grad.reshape(local_spans, SEG, groups, QPG, HD)  2.98 us
  transfers between devices with their start and end apart: 2, of which 1 were waited for; matrix products, arithmetic and copies ran while one was open for 33% of the time, Pallas kernels for 0%

profile of v1, /device:TPU:0, one launch (start us, length us, event | category | flops | bytes accessed | tf_op | source)
XLA Modules:
  0.0 128.3 jit_solution(9557685229472989318)
XLA Ops:
  8.5 6.3 %all-to-all-start = ((bf16[4,32,256]{2,1,0:T(8,128)(2,1)}), bf16[4,32,256]{2,1,0:T(8,128)(2,1)S(1)}, u32[]{:S(2)}, u32[]{:S(2)}) async-start(bf16[4,32,256]{2,1,0:T(8,128)(2,1)} %stack.61), calls=%async_computation | async-start | bytes 131072 | tf_op jit(solution)/shard_map/all_to_all | solution.py:120
  14.9 1.2 dynamic_slice.3
  19.6 2.2 %reshape.1314 = bf16[1,544,1,7,128]{4,3,1,2,0:T(8,128)(2,1)S(1)} reshape(bf16[544,896]{1,0:T(8,128)(2,1)} %param.5) | data formatting | bytes 1949696 | tf_op jit(solution)/shard_map/reshape | solution.py:108
  21.8 2.4 %fusion.265 = (bf16[1,544,1,1,128]{4,3,1,2,0:T(2,128)(2,1)S(1)}, bf16[1,544,1,1,128]{4,3,1,2,0:T(2,128)(2,1)S(1)}, bf16[1,544,1,1,128]{4,3,1,2,0:T(2,128)(2,1)},...) fusion(bf16[1,544,1,7,128]{4,3,1,2,0:T(8,128)(2,1)S(1)} %reshap, ...), kind=kLoop, calls=%fused_computation.404 | loop fusion | bytes 1949696 | tf_op jit(solution)/shard_map/slice | solution.py:142
  24.9 1.2 fusion.280
  26.2 1.2 fusion.278
  27.4 2.5 %fusion.276 = (f32[544]{0:T(1024)}, f32[544,544]{0,1:T(8,128)}) fusion(bf16[544,128]{1,0:T(8,128)(2,1)S(1)} %copy-done.6, bf16[1,544,1,1,128]{4,1,3,2,0:T(8,128)(2,1)S(1)} %copy.70, pred[544]{0:T(1024)(128)(4,1)S(1)} %get-tuple-element.81, pred[544]{0:T(1024)(128)(4,1)S(1)} %get-tuple-element.80, s32[544]{0:T(1024)S(1)} %iota_select_fusion, ...), kind=kOutput, calls=%fused_computation.415 | convolution fusion | flops 78718432 | bytes 1468256 | tf_op jit(solution)/shard_map/csd,ctd->cst/dot_general | solution.py:15
  30.0 3.5 %fusion.274 = (f32[544]{0:T(1024)}, f32[544,544]{0,1:T(8,128)}) fusion(bf16[544,128]{1,0:T(8,128)(2,1)S(1)} %copy-done.6, bf16[1,544,1,1,128]{4,1,3,2,0:T(8,128)(2,1)S(1)} %copy.69, pred[544]{0:T(1024)(128)(4,1)} %copy-done.54, pred[544]{0:T(1024)(128)(4,1)S(1)} %get-tuple-element.80, s32[544]{0:T(1024)S(1)} %iota_select_fusion, pred[544]{0:T(1024)(128)(4,1)} %copy-done.56), kind=kOutput, calls=%fused_computation.413 | convolution fusion | flops 78718432 | bytes 1468256 | tf_op jit(solution)/shard_map/csd,ctd->cst/dot_general | solution.py:15
  33.5 2.5 %fusion.272 = (f32[544]{0:T(1024)}, f32[544,544]{0,1:T(8,128)}) fusion(bf16[544,128]{1,0:T(8,128)(2,1)S(1)} %copy-done.6, bf16[1,544,1,1,128]{4,1,3,2,0:T(8,128)(2,1)S(1)} %copy.68, pred[544]{0:T(1024)(128)(4,1)S(1)} %copy-done.55, pred[544]{0:T(1024)(128)(4,1)S(1)} %get-tuple-element.80, s32[544]{0:T(1024)S(1)} %iota_select_fusion, ...), kind=kOutput, calls=%fused_computation.411 | convolution fusion | flops 78718432 | bytes 1468256 | tf_op jit(solution)/shard_map/csd,ctd->cst/dot_general | solution.py:15
  36.1 2.5 %fusion.270 = (f32[544]{0:T(1024)}, f32[544,544]{0,1:T(8,128)}) fusion(bf16[544,128]{1,0:T(8,128)(2,1)S(1)} %copy-done.6, bf16[1,544,1,1,128]{4,1,3,2,0:T(8,128)(2,1)S(1)} %copy.67, pred[544]{0:T(1024)(128)(4,1)S(1)} %copy-done.55, pred[544]{0:T(1024)(128)(4,1)S(1)} %get-tuple-element.80, s32[544]{0:T(1024)S(1)} %iota_select_fusion, ...), kind=kOutput, calls=%fused_computation.409 | convolution fusion | flops 78718432 | bytes 1468256 | tf_op jit(solution)/shard_map/csd,ctd->cst/dot_general | solution.py:15
  38.6 2.5 %fusion.268 = (f32[544]{0:T(1024)}, f32[544,544]{0,1:T(8,128)}) fusion(bf16[544,128]{1,0:T(8,128)(2,1)S(1)} %copy-done.6, bf16[1,544,1,1,128]{4,1,3,2,0:T(8,128)(2,1)S(1)} %copy.66, pred[544]{0:T(1024)(128)(4,1)S(1)} %copy-done.55, pred[544]{0:T(1024)(128)(4,1)S(1)} %get-tuple-element.80, s32[544]{0:T(1024)S(1)} %iota_select_fusion, ...), kind=kOutput, calls=%fused_computation.407 | convolution fusion | flops 78718432 | bytes 1468256 | tf_op jit(solution)/shard_map/csd,ctd->cst/dot_general | solution.py:15
  41.1 3.0 %reshape.1322 = bf16[1,544,1,7,128]{4,3,1,2,0:T(8,128)(2,1)} reshape(bf16[544,896]{1,0:T(8,128)(2,1)} %param.8) | data formatting | bytes 1949696 | tf_op jit(solution)/shard_map/reshape | solution.py:109
  44.1 6.8 %fusion.264 = (bf16[1,544,1,1,128]{4,3,1,2,0:T(2,128)(2,1)}, bf16[1,544,1,1,128]{4,3,1,2,0:T(2,128)(2,1)}, bf16[1,544,1,1,128]{4,3,1,2,0:T(2,128)(2,1)}, bf16[1,...) fusion(bf16[1,544,1,7,128]{4,3,1,2,0:T(8,128)(2,1)} %reshape.1322), kind=kLoop, calls=%fused_computation.403 | loop fusion | bytes 1949696 | tf_op jit(solution)/shard_map/slice | solution.py:143
  51.0 1.0 fusion.279
  52.0 1.0 fusion.277
  52.9 1.0 fusion.275
  53.9 1.0 fusion.273
  54.9 1.0 fusion.271
  55.9 1.0 fusion.269
  56.8 1.0 fusion.267
  67.8 0.9 copy-done.24
  68.7 0.9 multiply_reduce_fusion
  70.9 1.3 %fusion.22 = bf16[544,544]{0,1:T(8,128)(2,1)} fusion(bf16[544,128]{1,0:T(8,128)(2,1)S(1)} %copy-done, f32[544,544]{0,1:T(8,128)S(1)} %copy-done.5, f32[544]{0:T(1024)S(1)} %get-tuple-element.5, f32[544]{0:T(1024)S(1)} %log_add_fusion.6, bf16[1,544,1,1,128]{4,1,3,2,0:T(8,128)(2,1)S(1)} %get-tuple-element.16, bf16[544]{0:T(1024)(128)(2,1)S(1)} %get-tuple-element.76), kind=kOutput, calls=%fused_computation.51 | convolution fusion | flops 77012992 | bytes 2059584 | tf_op jit(solution)/shard_map/csd,ctd->cst/dot_general | solution.py:15
  72.5 1.3 %fusion.21 = bf16[544,544]{0,1:T(8,128)(2,1)} fusion(bf16[544,128]{1,0:T(8,128)(2,1)S(1)} %copy-done, f32[544,544]{0,1:T(8,128)S(1)} %copy-done.4, f32[544]{0:T(1024)S(1)} %get-tuple-element.6, f32[544]{0:T(1024)S(1)} %log_add_fusion.5, bf16[1,544,1,1,128]{4,1,3,2,0:T(8,128)(2,1)S(1)} %get-tuple-element.15, bf16[544]{0:T(1024)(128)(2,1)S(1)} %get-tuple-element.76), kind=kOutput, calls=%fused_computation.50 | convolution fusion | flops 77012992 | bytes 2059584 | tf_op jit(solution)/shard_map/csd,ctd->cst/dot_general | solution.py:15
  74.1 1.3 %fusion.20 = bf16[544,544]{0,1:T(8,128)(2,1)} fusion(bf16[544,128]{1,0:T(8,128)(2,1)S(1)} %copy-done, f32[544,544]{0,1:T(8,128)S(1)} %copy-done.3, f32[544]{0:T(1024)S(1)} %get-tuple-element.7, f32[544]{0:T(1024)S(1)} %log_add_fusion.4, bf16[1,544,1,1,128]{4,1,3,2,0:T(8,128)(2,1)S(1)} %get-tuple-element.14, bf16[544]{0:T(1024)(128)(2,1)S(1)} %get-tuple-element.76), kind=kOutput, calls=%fused_computation.49 | convolution fusion | flops 77012992 | bytes 2059584 | tf_op jit(solution)/shard_map/csd,ctd->cst/dot_general | solution.py:15
  76.0 1.3 %fusion.19 = bf16[544,544]{0,1:T(8,128)(2,1)} fusion(bf16[544,128]{1,0:T(8,128)(2,1)S(1)} %copy-done, f32[544,544]{0,1:T(8,128)S(1)} %copy-done.2, f32[544]{0:T(1024)S(1)} %get-tuple-element.8, f32[544]{0:T(1024)S(1)} %log_add_fusion.3, bf16[1,544,1,1,128]{4,1,3,2,0:T(8,128)(2,1)S(1)} %get-tuple-element.13, bf16[544]{0:T(1024)(128)(2,1)S(1)} %get-tuple-element.76), kind=kOutput, calls=%fused_computation.48 | convolution fusion | flops 77012992 | bytes 2059584 | tf_op jit(solution)/shard_map/csd,ctd->cst/dot_general | solution.py:15
  77.6 1.4 %fusion.18 = bf16[544,544]{0,1:T(8,128)(2,1)} fusion(bf16[544,128]{1,0:T(8,128)(2,1)S(1)} %copy-done, f32[544,544]{0,1:T(8,128)S(1)} %copy-done.1, f32[544]{0:T(1024)S(1)} %get-tuple-element.9, f32[544]{0:T(1024)S(1)} %log_add_fusion.2, bf16[1,544,1,1,128]{4,1,3,2,0:T(8,128)(2,1)S(1)} %get-tuple-element.12, bf16[544]{0:T(1024)(128)(2,1)S(1)} %get-tuple-element.76), kind=kOutput, calls=%fused_computation.47 | convolution fusion | flops 77012992 | bytes 2059584 | tf_op jit(solution)/shard_map/csd,ctd->cst/dot_general | solution.py:15
  79.3 1.3 %fusion.17 = bf16[544,544]{0,1:T(8,128)(2,1)} fusion(bf16[544,128]{1,0:T(8,128)(2,1)S(1)} %copy-done, f32[544,544]{0,1:T(8,128)S(1)} %get-tuple-element.67, f32[544]{0:T(1024)S(1)} %get-tuple-element.10, f32[544]{0:T(1024)S(1)} %log_add_fusion.1, bf16[1,544,1,1,128]{4,1,3,2,0:T(8,128)(2,1)S(1)} %get-tuple-element.11, bf16[544]{0:T(1024)(128)(2,1)S(1)} %get-tuple-element.76), kind=kOutput, calls=%fused_computation.46 | convolution fusion | flops 77012992 | bytes 2059584 | tf_op jit(solution)/shard_map/csd,ctd->cst/dot_general | solution.py:15
  80.9 1.3 %fusion.16 = bf16[544,544]{0,1:T(8,128)(2,1)} fusion(bf16[544,128]{1,0:T(8,128)(2,1)S(1)} %copy-done, f32[544,544]{0,1:T(8,128)S(1)} %get-tuple-element.73, f32[544]{0:T(1024)S(1)} %get-tuple-element.4, f32[544]{0:T(1024)S(1)} %log_add_fusion, bf16[1,544,1,1,128]{4,1,3,2,0:T(8,128)(2,1)S(1)} %get-tuple-element.17, bf16[544]{0:T(1024)(128)(2,1)S(1)} %get-tuple-element.76), kind=kOutput, calls=%fused_computation.45 | convolution fusion | flops 77012992 | bytes 2059584 | tf_op jit(solution)/shard_map/csd,ctd->cst/dot_general | solution.py:15
  105.0 1.1 copy.93
  106.9 1.1 copy.94
  108.0 10.3 %reduce-scatter.4.cloned.1.call-done = f32[32,256]{1,0:T(8,128)} async-done(((f32[128,256]{1,0:T(8,128)}), f32[32,256]{1,0:T(8,128)}) %reduce-scatter.4.cloned.1.call-update) | async-done | bytes 32784
  (241 shorter events, 42.8 us)
Async XLA Ops:
  8.5 42.4 %all-to-all-start = ((bf16[4,32,256]{2,1,0:T(8,128)(2,1)}), bf16[4,32,256]{2,1,0:T(8,128)(2,1)S(1)}, u32[]{:S(2)}, u32[]{:S(2)}) async-start(bf16[4,32,256]{2,1,0:T(8,128)(2,1)} %stack.61), calls=%async_computation | async-start | bytes 131072 | tf_op jit(solution)/shard_map/all_to_all | solution.py:120
  14.9 103.5 %reduce-scatter.4.cloned.1.call-start = ((), (), s32[]{:S(2)}) async-start(), calls=%async_computation.2 | async-start | bytes 163840
  18.1 9.3 %copy-start.56 = (pred[544]{0:T(1024)(128)(4,1)}, pred[544]{0:T(1024)(128)(4,1)S(1)}, u32[]{:S(2)}) copy-start(pred[544]{0:T(1024)(128)(4,1)S(1)} %fusion.220) | copy-start | bytes 1636
  18.9 8.5 %copy-start.54 = (pred[544]{0:T(1024)(128)(4,1)}, pred[544]{0:T(1024)(128)(4,1)S(1)}, u32[]{:S(2)}) copy-start(pred[544]{0:T(1024)(128)(4,1)S(1)} %get-tuple-element.81) | copy-start | bytes 1636
  21.8 3.2 %copy-start.6 = (bf16[544,128]{1,0:T(8,128)(2,1)S(1)}, bf16[544,128]{1,0:T(8,128)(2,1)}, u32[]{:S(2)}) copy-start(bf16[544,128]{1,0:T(8,128)(2,1)} %param.6) | copy-start | bytes 417796
  27.4 2.5 %copy-start.43 = (bf16[1,544,1,1,128]{4,3,1,2,0:T(2,128)(2,1)S(1)}, bf16[1,544,1,1,128]{4,3,1,2,0:T(2,128)(2,1)}, u32[]{:S(2)}) copy-start(bf16[1,544,1,1,128]{4,3,1,2,0:T(2,128)(2,1)} %get-tuple-element.28) | copy-start | bytes 417796
  29.9 3.5 %copy-start.15 = (bf16[1,544,1,1,128]{4,1,3,2,0:T(8,128)(2,1)}, bf16[1,544,1,1,128]{4,1,3,2,0:T(8,128)(2,1)S(1)}, u32[]{:S(2)}) copy-start(bf16[1,544,1,1,128]{4,1,3,2,0:T(8,128)(2,1)S(1)} %copy.69) | copy-start | bytes 417796
  30.0 3.5 %copy-start.42 = (bf16[1,544,1,1,128]{4,3,1,2,0:T(2,128)(2,1)S(1)}, bf16[1,544,1,1,128]{4,3,1,2,0:T(2,128)(2,1)}, u32[]{:S(2)}) copy-start(bf16[1,544,1,1,128]{4,3,1,2,0:T(2,128)(2,1)} %get-tuple-element.29) | copy-start | bytes 417796
  30.0 3.5 %copy-start.55 = (pred[544]{0:T(1024)(128)(4,1)S(1)}, pred[544]{0:T(1024)(128)(4,1)}, u32[]{:S(2)}) copy-start(pred[544]{0:T(1024)(128)(4,1)} %copy-done.54) | copy-start | bytes 1636
  30.0 3.5 %copy-start.57 = (pred[544]{0:T(1024)(128)(4,1)S(1)}, pred[544]{0:T(1024)(128)(4,1)}, u32[]{:S(2)}) copy-start(pred[544]{0:T(1024)(128)(4,1)} %copy-done.56) | copy-start | bytes 1636
  33.5 2.5 %copy-start.18 = (bf16[1,544,1,1,128]{4,1,3,2,0:T(8,128)(2,1)}, bf16[1,544,1,1,128]{4,1,3,2,0:T(8,128)(2,1)S(1)}, u32[]{:S(2)}) copy-start(bf16[1,544,1,1,128]{4,1,3,2,0:T(8,128)(2,1)S(1)} %copy.68) | copy-start | bytes 417796
  33.5 2.5 %copy-start.41 = (bf16[1,544,1,1,128]{4,3,1,2,0:T(2,128)(2,1)S(1)}, bf16[1,544,1,1,128]{4,3,1,2,0:T(2,128)(2,1)}, u32[]{:S(2)}) copy-start(bf16[1,544,1,1,128]{4,3,1,2,0:T(2,128)(2,1)} %get-tuple-element.30) | copy-start | bytes 417796
  36.1 2.5 %copy-start.21 = (bf16[1,544,1,1,128]{4,1,3,2,0:T(8,128)(2,1)}, bf16[1,544,1,1,128]{4,1,3,2,0:T(8,128)(2,1)S(1)}, u32[]{:S(2)}) copy-start(bf16[1,544,1,1,128]{4,1,3,2,0:T(8,128)(2,1)S(1)} %copy.67) | copy-start | bytes 417796
  36.1 2.5 %copy-start.40 = (bf16[1,544,1,1,128]{4,3,1,2,0:T(2,128)(2,1)S(1)}, bf16[1,544,1,1,128]{4,3,1,2,0:T(2,128)(2,1)}, u32[]{:S(2)}) copy-start(bf16[1,544,1,1,128]{4,3,1,2,0:T(2,128)(2,1)} %get-tuple-element.31) | copy-start | bytes 417796
  50.9 3.0 %copy-start.16 = (bf16[1,544,1,1,128]{4,1,3,2,0:T(8,128)(2,1)S(1)}, bf16[1,544,1,1,128]{4,1,3,2,0:T(8,128)(2,1)}, u32[]{:S(2)}) copy-start(bf16[1,544,1,1,128]{4,1,3,2,0:T(8,128)(2,1)} %copy-done.15) | copy-start | bytes 417796
  50.9 3.9 %copy-start.19 = (bf16[1,544,1,1,128]{4,1,3,2,0:T(8,128)(2,1)S(1)}, bf16[1,544,1,1,128]{4,1,3,2,0:T(8,128)(2,1)}, u32[]{:S(2)}) copy-start(bf16[1,544,1,1,128]{4,1,3,2,0:T(8,128)(2,1)} %copy-done.18) | copy-start | bytes 417796
  51.0 4.9 %copy-start.22 = (bf16[1,544,1,1,128]{4,1,3,2,0:T(8,128)(2,1)S(1)}, bf16[1,544,1,1,128]{4,1,3,2,0:T(8,128)(2,1)}, u32[]{:S(2)}) copy-start(bf16[1,544,1,1,128]{4,1,3,2,0:T(8,128)(2,1)} %copy-done.21) | copy-start | bytes 417796
  52.0 5.8 %copy-start.53 = (f32[544]{0:T(1024)S(1)}, f32[544]{0:T(1024)}, u32[]{:S(2)}) copy-start(f32[544]{0:T(1024)} %get-tuple-element.72) | copy-start | bytes 6532
  56.8 1.8 %copy-start.52 = (f32[544]{0:T(1024)S(1)}, f32[544]{0:T(1024)}, u32[]{:S(2)}) copy-start(f32[544]{0:T(1024)} %get-tuple-element.66) | copy-start | bytes 6532
  67.2 1.5 %copy-start.33 = (bf16[1,544,1,1,128]{4,3,1,2,0:T(2,128)(2,1)S(1)}, bf16[1,544,1,1,128]{4,3,1,2,0:T(2,128)(2,1)}, u32[]{:S(2)}) copy-start(bf16[1,544,1,1,128]{4,3,1,2,0:T(2,128)(2,1)} %get-tuple-element.18) | copy-start | bytes 417796
  67.2 1.5 %copy-start.34 = (bf16[1,544,1,1,128]{4,3,1,2,0:T(2,128)(2,1)S(1)}, bf16[1,544,1,1,128]{4,3,1,2,0:T(2,128)(2,1)}, u32[]{:S(2)}) copy-start(bf16[1,544,1,1,128]{4,3,1,2,0:T(2,128)(2,1)} %get-tuple-element.19) | copy-start | bytes 417796
  67.2 1.5 %copy-start.35 = (bf16[1,544,1,1,128]{4,3,1,2,0:T(2,128)(2,1)S(1)}, bf16[1,544,1,1,128]{4,3,1,2,0:T(2,128)(2,1)}, u32[]{:S(2)}) copy-start(bf16[1,544,1,1,128]{4,3,1,2,0:T(2,128)(2,1)} %get-tuple-element.20) | copy-start | bytes 417796
  67.2 1.5 %copy-start.36 = (bf16[1,544,1,1,128]{4,3,1,2,0:T(2,128)(2,1)S(1)}, bf16[1,544,1,1,128]{4,3,1,2,0:T(2,128)(2,1)}, u32[]{:S(2)}) copy-start(bf16[1,544,1,1,128]{4,3,1,2,0:T(2,128)(2,1)} %get-tuple-element.21) | copy-start | bytes 417796
  67.2 1.5 %copy-start.37 = (bf16[1,544,1,1,128]{4,3,1,2,0:T(2,128)(2,1)S(1)}, bf16[1,544,1,1,128]{4,3,1,2,0:T(2,128)(2,1)}, u32[]{:S(2)}) copy-start(bf16[1,544,1,1,128]{4,3,1,2,0:T(2,128)(2,1)} %get-tuple-element.22) | copy-start | bytes 417796
  67.3 1.5 %copy-start.38 = (bf16[1,544,1,1,128]{4,3,1,2,0:T(2,128)(2,1)S(1)}, bf16[1,544,1,1,128]{4,3,1,2,0:T(2,128)(2,1)}, u32[]{:S(2)}) copy-start(bf16[1,544,1,1,128]{4,3,1,2,0:T(2,128)(2,1)} %get-tuple-element.23) | copy-start | bytes 417796
  67.3 1.5 %copy-start.39 = (bf16[1,544,1,1,128]{4,3,1,2,0:T(2,128)(2,1)S(1)}, bf16[1,544,1,1,128]{4,3,1,2,0:T(2,128)(2,1)}, u32[]{:S(2)}) copy-start(bf16[1,544,1,1,128]{4,3,1,2,0:T(2,128)(2,1)} %get-tuple-element.24) | copy-start | bytes 417796
  86.1 4.2 %copy-start.45 = (f32[1,544,1,128]{3,1,2,0:T(8,128)}, f32[1,544,1,128]{3,1,2,0:T(8,128)S(1)}, u32[]{:S(2)}) copy-start(f32[1,544,1,128]{3,1,2,0:T(8,128)S(1)} %fusion.30) | copy-start | bytes 835588
  94.7 2.6 %copy-start.7 = (bf16[544,544]{0,1:T(8,128)(2,1)S(1)}, bf16[544,544]{0,1:T(8,128)(2,1)}, u32[]{:S(2)}) copy-start(bf16[544,544]{0,1:T(8,128)(2,1)} %fusion.22) | copy-start | bytes 1775620
  95.6 2.1 %copy-start.26 = (f32[544,128]{1,0:T(8,128)S(1)}, f32[544,128]{1,0:T(8,128)}, u32[]{:S(2)}) copy-start(f32[544,128]{1,0:T(8,128)} %fusion.255) | copy-start | bytes 835588
  96.5 1.6 %copy-start.13 = (bf16[544,544]{0,1:T(8,128)(2,1)S(1)}, bf16[544,544]{0,1:T(8,128)(2,1)}, u32[]{:S(2)}) copy-start(bf16[544,544]{0,1:T(8,128)(2,1)} %fusion.21) | copy-start | bytes 1775620
  96.5 1.6 %copy-start.23 = (bf16[1,544,1,1,128]{4,1,3,2,0:T(8,128)(2,1)S(1)}, bf16[1,544,1,1,128]{4,1,3,2,0:T(8,128)(2,1)}, u32[]{:S(2)}) copy-start(bf16[1,544,1,1,128]{4,1,3,2,0:T(8,128)(2,1)} %copy-done.21) | copy-start | bytes 417796
  106.9 13.2 %copy-start.46 = (bf16[512,128]{1,0:T(8,128)(2,1)S(1)}, bf16[512,128]{1,0:T(8,128)(2,1)}, u32[]{:S(2)}) copy-start(bf16[512,128]{1,0:T(8,128)(2,1)} %fusion.165) | copy-start | bytes 393220
  (28 other events, 33.9 us)
Sparse Core Ops, SparseCore 0:
  97.4 20.8 reduce-scatter.3
